TPU v7x, 128 devices: a whole 4x4x4 slice. The times are simulated.
128 devices in a mesh: dp: 4 (over z), expert: 32 (over y, x, core).
Axes of the slice: x: 4, y: 4, z: 4, core: 2. Of those that a mesh axis runs over, the one named last changes fastest.
Arguments:
- tokens: bfloat16 [16384, 2048], P(('dp', 'expert')), may hold values from -6 to 6
- out_grad: bfloat16 [16384, 2048], P(('dp', 'expert')), may hold values from -6 to 6
- gate_saved: bfloat16 [16384, 6, 1408], P(('dp', 'expert')), may hold values from -6 to 6
- probs: float32 [16384, 6], P(('dp', 'expert')), may hold values from 0.1 to 1
- expert_ids: int32 [16384, 6], P(('dp', 'expert')), may hold values from 0 to 31, all different within a row; in each aligned block of 128 rows (0 to 127, 128 to 255, ...) at most 48 rows name the same one
- w_gate: bfloat16 [32, 2048, 1408], P('expert'), may hold values from -0.125 to 0.125
- w_up: bfloat16 [32, 2048, 1408], P('expert'), may hold values from -0.125 to 0.125
- w_down: bfloat16 [32, 1408, 2048], P('expert'), may hold values from -0.15625 to 0.15625
Outputs:
- input_grad: bfloat16 [16384, 2048], P(('dp', 'expert'))
- grad_gate: bfloat16 [32, 2048, 1408], P('expert', 'dp')
- grad_up: bfloat16 [32, 2048, 1408], P('expert', 'dp')
- grad_down: bfloat16 [32, 1408, 2048], P('expert', 'dp')
Inputs may be any that keep to these rules, and one draw needn't show every extreme that they name: `expert_ids`: each token names 6 different experts. Among the 128 tokens of one aligned block (the tokens of one device) no expert is named more than 48 times, and in some block some expert is named exactly 48 times.
All inputs are finite; a program needn't handle non-finite values.
Results may differ from a plain program's by a relative error of at most 0.013.
Values may be sent and summed in bfloat16 or wider, within the bound.
A program may use at most 192 MiB of HBM per device.

v0:
```python
import jax
import jax.numpy as jnp
from jax import lax
from jax.sharding import PartitionSpec as P

grad_scale = 0.0625
slot_cap = 48
gate_cuts = (0, 384, 896, 1408)


def mm(a, b, ca, cb):
    return lax.dot_general(a, b, (((ca,), (cb,)), ((), ())), preferred_element_type=jnp.float32)


def slot_onehot(chosen):
    n_tok = chosen.shape[1]
    before = (
        lax.broadcasted_iota(jnp.int32, (n_tok, n_tok), 0)
        < lax.broadcasted_iota(jnp.int32, (n_tok, n_tok), 1)
    ).astype(jnp.bfloat16)
    rank = mm(chosen.astype(jnp.bfloat16), before, 1, 0).astype(jnp.int32)
    slots = lax.broadcasted_iota(jnp.int32, (1, slot_cap, 1), 1)
    return (rank[:, None, :] == slots) & chosen[:, None, :]


def local(tokens, out_grad, gate_saved, probs, expert_ids, w_gate, w_up, w_down):
    n_peers = lax.axis_size("expert")
    me = lax.axis_index("expert")
    tok_rows, model_width = tokens.shape
    top_k = expert_ids.shape[1]
    hidden_width = w_up.shape[2]
    n_slots = n_peers * slot_cap
    gate_mat, up_mat, down_mat = (w_gate[0], w_up[0], w_down[0])
    meta = jnp.concatenate([expert_ids.T.astype(jnp.float32), probs.T], axis=0)
    meta_all = lax.all_gather(meta, "expert", axis=0, tiled=False)
    rows_all = lax.all_gather(tokens, "expert", axis=0, tiled=True)
    grad_all = lax.all_gather(out_grad, "expert", axis=0, tiled=True)
    ids_t = expert_ids.T
    experts = lax.broadcasted_iota(jnp.int32, (n_peers, 1, 1), 0)
    named = ids_t[None] == experts
    send_hot = slot_onehot(jnp.any(named, axis=1))
    toks = lax.broadcasted_iota(jnp.int32, (1, top_k, tok_rows), 2)
    ks = lax.broadcasted_iota(jnp.int32, (1, top_k, tok_rows), 1)
    route_of = jnp.sum(jnp.where(named, toks * top_k + ks, 0), axis=1)
    route_of_slot = jnp.sum(jnp.where(send_hot, route_of[:, None, :], 0), axis=2)
    gate_rows = gate_saved.reshape(tok_rows * top_k, hidden_width)[route_of_slot.reshape(n_slots)]
    gate_rows = gate_rows.reshape(n_peers, slot_cap, hidden_width)
    recv_gate = [
        lax.all_to_all(
            gate_rows[:, :, a:b], "expert", split_axis=0, concat_axis=0, tiled=True
        ).reshape(n_slots, b - a)
        for a, b in zip(gate_cuts, gate_cuts[1:])
    ]
    mine = meta_all[:, :top_k, :] == me.astype(jnp.float32)
    prob_of = jnp.sum(jnp.where(mine, meta_all[:, top_k:, :], 0.0), axis=1)
    recv_hot = slot_onehot(jnp.any(mine, axis=1))
    tok_ids = lax.broadcasted_iota(jnp.int32, (1, 1, tok_rows), 2)
    src = lax.broadcasted_iota(jnp.int32, (n_peers, slot_cap), 0)
    row_of_slot = (src * tok_rows + jnp.sum(jnp.where(recv_hot, tok_ids, 0), axis=2)).reshape(
        n_slots
    )
    prob_of_slot = jnp.sum(jnp.where(recv_hot, prob_of[:, None, :], 0.0), axis=2).reshape(n_slots)
    used = jnp.any(recv_hot, axis=2).reshape(n_slots)
    rows_in = jnp.where(used[:, None], rows_all[row_of_slot], 0)
    routed = (prob_of_slot[:, None] * grad_all[row_of_slot].astype(jnp.float32)).astype(
        jnp.bfloat16
    )
    shares = []
    hidden, part = ([], None)
    for j, (a, b) in enumerate(zip(gate_cuts, gate_cuts[1:])):
        up_act = mm(rows_in, up_mat[:, a:b], 1, 0)
        hidden_grad = mm(routed, down_mat[a:b, :], 1, 1)
        gate_val = recv_gate[j].astype(jnp.float32)
        gate_sig = jax.nn.sigmoid(gate_val)
        gate_act = gate_val * gate_sig
        hidden.append((gate_act * up_act).astype(jnp.bfloat16))
        up_grad = (hidden_grad * gate_act).astype(jnp.bfloat16)
        gate_grad = (hidden_grad * up_act * gate_sig * (1.0 + gate_val * (1.0 - gate_sig))).astype(
            jnp.bfloat16
        )
        both = jnp.concatenate([gate_grad, up_grad], axis=1)
        term = mm(rows_in, both, 0, 0).astype(jnp.bfloat16)
        shares.append(lax.psum_scatter(term, "dp", scatter_dimension=0, tiled=True))
        piece = mm(gate_grad, gate_mat[:, a:b], 1, 1) + mm(up_grad, up_mat[:, a:b], 1, 1)
        part = piece if part is None else part + piece
    hidden_act = jnp.concatenate(hidden, axis=1)
    term_down = mm(hidden_act, routed, 0, 0).astype(jnp.bfloat16)
    share_down = lax.psum_scatter(term_down, "dp", scatter_dimension=0, tiled=True)
    back = part.astype(jnp.bfloat16).reshape(n_peers, slot_cap, model_width)
    returned = lax.all_to_all(back, "expert", split_axis=0, concat_axis=0, tiled=True)
    input_grad = mm(
        send_hot.reshape(n_slots, tok_rows).astype(jnp.bfloat16),
        returned.reshape(n_slots, model_width),
        0,
        0,
    ).astype(jnp.bfloat16)

    def scaled(share):
        return (grad_scale * share.astype(jnp.float32)).astype(jnp.bfloat16)

    widths = [b - a for a, b in zip(gate_cuts, gate_cuts[1:])]
    grad_gate = jnp.concatenate([scaled(s[:, :w]) for s, w in zip(shares, widths)], axis=1)[None]
    grad_up = jnp.concatenate([scaled(s[:, w:]) for s, w in zip(shares, widths)], axis=1)[None]
    return (input_grad, grad_gate, grad_up, scaled(share_down)[None])


def solution(mesh):
    return jax.shard_map(
        local,
        mesh=mesh,
        in_specs=(
            P(("dp", "expert"), None),
            P(("dp", "expert"), None),
            P(("dp", "expert"), None, None),
            P(("dp", "expert"), None),
            P(("dp", "expert"), None),
            P("expert", None, None),
            P("expert", None, None),
            P("expert", None, None),
        ),
        out_specs=(
            P(("dp", "expert"), None),
            P("expert", "dp", None),
            P("expert", "dp", None),
            P("expert", "dp", None),
        ),
        check_vma=False,
    )
```

profile of v0, /device:TPU:1, one launch (start us, length us, event | category | flops | bytes accessed | tf_op | source)
XLA Modules:
  0.0 478.7 jit_solution(1710951057539450567)
XLA Ops:
  7.2 0.7 all-gather.5.cloned.1.call-update
  7.9 0.7 all-gather.7.cloned.1.call-update
  8.7 0.7 fusion.52
  9.4 0.7 select_reduce_fusion.3
  10.1 0.1 convolution_convert_fusion.5
  10.2 0.6 copy-done.9
  10.8 0.6 select_reduce_fusion
  11.6 4.4 copy.36
  16.0 3.6 reshape.119
  19.6 6.2 %gather_fusion.2 = bf16[1536,1408]{1,0:T(8,128)(2,1)} fusion(bf16[768,1408]{1,0:T(8,128)(2,1)S(1)} %reshape.119, s32[2048]{0:T(1024)S(1)} %pad_clamp_fusion), kind=kCustom, calls=%fused_computation.2 | custom fusion | bytes 8656896 | tf_op jit(solution)/shard_map/gather | solution.py:46
  25.8 2.4 slice.104
  28.2 8.6 %all-to-all-start = ((bf16[32,48,384]{2,1,0:T(8,128)(2,1)}), bf16[32,48,384]{2,1,0:T(8,128)(2,1)S(1)}, u32[]{:S(2)}, u32[]{:S(2)}) async-start(bf16[32,48,384]{2,1,0:T(8,128)(2,1)} %slice.104), calls=%async_computation | async-start | bytes 2359296 | tf_op jit(solution)/shard_map/all_to_all | solution.py:49
  36.9 37.6 %all-gather.1 = f32[32,12,128]{2,1,0:T(8,128)S(1)} all-gather(f32[1,12,128]{2,1,0:T(8,128)S(1)} %maximum_bitcast_fusion.2), channel_id=2, replica_groups=mesh['dp'=4,'expert'=32] {'expert'}, dimensions={0}, use_global_device_ids=true | all-gather | bytes 202752 | tf_op jit(solution)/shard_map/all_gather | solution.py:35
  74.6 0.1 convolution_convert_fusion.4
  74.7 0.3 select_reduce_fusion.2
  75.1 0.6 fusion.48
  75.7 0.7 broadcast_in_dim.88
  76.4 0.6 select_reduce_fusion.1
  77.3 4.2 fusion.59
  81.4 5.2 %all-to-all-start.1 = ((bf16[32,48,512]{2,1,0:T(8,128)(2,1)}), bf16[32,48,512]{2,1,0:T(8,128)(2,1)}, u32[]{:S(2)}, u32[]{:S(2)}) async-start(bf16[32,48,512]{2,1,0:T(8,128)(2,1)} %get-tuple-element.15), calls=%async_computation.1 | async-start | bytes 3145728 | tf_op jit(solution)/shard_map/all_to_all | solution.py:49
  86.6 0.3 reduce-scatter.5.cloned.1.call-start
  86.9 0.3 bitcast_convert_fusion.2
  87.2 2.0 copy.37
  89.2 1.2 all-gather.5.cloned.1.call-done
  90.4 20.6 %gather_fusion = bf16[1536,2048]{1,0:T(8,128)(2,1)} fusion(bf16[4096,2048]{1,0:T(8,128)(2,1)} %all-gather.5.cloned.1.call-done, s32[2048]{0:T(1024)S(1)} %pad_clamp_fusion.1), kind=kCustom, calls=%fused_computation | custom fusion | bytes 12589056 | tf_op jit(solution)/shard_map/gather | solution.py:65
  111.1 7.5 %fusion.38 = f32[1536,384]{0,1:T(8,128)} fusion(bf16[1,1408,2048]{2,1,0:T(8,128)(2,1)} %param.15, bf16[1536,2048]{1,0:T(8,128)(2,1)} %gather_fusion, f32[1536]{0:T(1024)S(1)} %mul.111), kind=kOutput, calls=%fused_computation.64 | convolution fusion | flops 2425356288 | bytes 10229760 | tf_op jit(solution)/shard_map/dot_general | solution.py:12
  118.6 49.0 %all-gather.7.cloned.1.call-done = bf16[4096,2048]{1,0:T(8,128)(2,1)} async-done(((bf16[128,2048]{1,0:T(8,128)(2,1)}), bf16[4096,2048]{1,0:T(8,128)(2,1)}) %all-gather.7.cloned.1.call-update) | async-done | bytes 16777232 | tf_op jit(solution)/shard_map/all_gather | solution.py:36
  167.5 20.6 %gather_fusion.1 = bf16[1536,2048]{1,0:T(8,128)(2,1)} fusion(bf16[4096,2048]{1,0:T(8,128)(2,1)} %all-gather.7.cloned.1.call-done, s32[2048]{0:T(1024)S(1)} %pad_clamp_fusion.1), kind=kCustom, calls=%fused_computation.1 | custom fusion | bytes 12589056 | tf_op jit(solution)/shard_map/gather | solution.py:64
  188.2 8.7 %multiply_convert_fusion.8 = (bf16[1536,384]{0,1:T(8,128)(2,1)}, bf16[1536,384]{0,1:T(8,128)(2,1)S(1)}, bf16[1536,384]{0,1:T(8,128)(2,1)S(1)}) fusion(f32[1536,384]{0,1:T(8,128)S(1)} %copy-done.4, f32[1536,384]{0,1:T(8,128)} %fusion.38, bf16[2048,1408]{1,0:T(8,128)(2,1)} %bitcast.58, bf16[1536,2048]{1,0:T(8,128)(2,1)} %gather_fusion.1, ...), kind=kOutput, calls=%fused_computation.37 | convolution fusion | flops 2427912192 | bytes 16123392 | tf_op jit(solution)/shard_map/dot_general | solution.py:12
  196.9 1.0 copy-done.5
  197.9 0.4 copy-done.7
  198.3 7.3 %convolution_convert_fusion.3 = bf16[2048,768]{1,0:T(8,128)(2,1)} fusion(bf16[1536,384]{0,1:T(8,128)(2,1)S(1)} %get-tuple-element.14, bf16[1536,384]{0,1:T(8,128)(2,1)S(1)} %get-tuple-element.13, bf16[1536,2048]{1,0:T(8,128)(2,1)S(1)} %copy-done.1, pred[1536]{0:T(1024)(128)(4,1)S(1)} %copy-done.15), kind=kOutput, calls=%fused_computation.14 | convolution fusion | flops 4841275392 | bytes 11798016 | tf_op jit(solution)/shard_map/dot_general | solution.py:12
  205.7 1.8 bitcast_convert_fusion.1
  207.5 2.6 copy.40
  210.1 6.6 %fusion.24 = f32[1536,512]{0,1:T(8,128)S(1)} fusion(bf16[1,1408,2048]{2,1,0:T(8,128)(2,1)} %param.15, bf16[1536,2048]{1,0:T(8,128)(2,1)} %gather_fusion, f32[1536]{0:T(1024)S(1)} %mul.111), kind=kOutput, calls=%fused_computation.48 | convolution fusion | flops 3230662656 | bytes 11540480 | tf_op jit(solution)/shard_map/dot_general | solution.py:12
  216.8 9.2 %multiply_convert_fusion.2 = (bf16[1536,512]{0,1:T(8,128)(2,1)}, bf16[1536,512]{0,1:T(8,128)(2,1)S(1)}, bf16[1536,512]{0,1:T(8,128)(2,1)S(1)}) fusion(f32[1536,512]{0,1:T(8,128)S(1)} %copy-done.2, f32[1536,512]{0,1:T(8,128)S(1)} %fusion.24, bf16[2048,1408]{1,0:T(8,128)(2,1)} %bitcast.59, bf16[1536,2048]{1,0:T(8,128)(2,1)} %gather_fusion.1, ...), kind=kOutput, calls=%fused_computation.22 | convolution fusion | flops 3236167680 | bytes 19400192 | tf_op jit(solution)/shard_map/dot_general | solution.py:12
  226.0 1.2 copy-done.16
  227.2 0.5 copy-done.18
  227.7 11.0 %convolution_convert_fusion.2 = bf16[2048,1024]{1,0:T(8,128)(2,1)} fusion(bf16[1536,512]{0,1:T(8,128)(2,1)S(1)} %get-tuple-element.8, bf16[1536,512]{0,1:T(8,128)(2,1)S(1)} %get-tuple-element.7, bf16[1536,2048]{1,0:T(8,128)(2,1)S(1)} %bitcast.52, pred[1536]{0:T(1024)(128)(4,1)S(1)} %copy-done.15), kind=kOutput, calls=%fused_computation.13 | convolution fusion | flops 6453985280 | bytes 13633024 | tf_op jit(solution)/shard_map/dot_general | solution.py:12
  238.8 1.4 copy-done
  240.2 28.2 %all_to_all.20 = bf16[32,48,512]{2,1,0:T(8,128)(2,1)S(1)} all-to-all(bf16[32,48,512]{2,1,0:T(8,128)(2,1)S(1)} %copy-done), channel_id=1, replica_groups=mesh['dp'=4,'expert'=32] {'expert'}, dimensions={0} | all-to-all | bytes 3145728 | tf_op jit(solution)/shard_map/all_to_all | solution.py:49
  268.4 0.5 bitcast_convert_fusion
  268.9 2.5 copy.43
  271.4 6.7 %fusion.22 = f32[1536,512]{0,1:T(8,128)S(1)} fusion(bf16[1,1408,2048]{2,1,0:T(8,128)(2,1)} %param.15, bf16[1536,2048]{1,0:T(8,128)(2,1)} %gather_fusion, f32[1536]{0:T(1024)S(1)} %mul.111), kind=kOutput, calls=%fused_computation.46 | convolution fusion | flops 3230662656 | bytes 11540480 | tf_op jit(solution)/shard_map/dot_general | solution.py:12
  278.1 9.2 %multiply_convert_fusion.1 = (bf16[1536,512]{0,1:T(8,128)(2,1)}, bf16[1536,512]{0,1:T(8,128)(2,1)S(1)}, bf16[1536,512]{0,1:T(8,128)(2,1)S(1)}) fusion(f32[1536,512]{0,1:T(8,128)S(1)} %copy-done.3, f32[1536,512]{0,1:T(8,128)S(1)} %fusion.22, bf16[2048,1408]{1,0:T(8,128)(2,1)} %bitcast.60, bf16[1536,2048]{1,0:T(8,128)(2,1)} %gather_fusion.1, ...), kind=kOutput, calls=%fused_computation.21 | convolution fusion | flops 3236167680 | bytes 19400192 | tf_op jit(solution)/shard_map/dot_general | solution.py:12
  287.4 1.2 copy-done.20
  288.5 0.5 copy-done.22
  289.0 11.0 %convolution_convert_fusion.1 = bf16[2048,1024]{1,0:T(8,128)(2,1)} fusion(bf16[1536,512]{0,1:T(8,128)(2,1)S(1)} %get-tuple-element.11, bf16[1536,512]{0,1:T(8,128)(2,1)S(1)} %get-tuple-element.10, bf16[1536,2048]{1,0:T(8,128)(2,1)S(1)} %bitcast.54, pred[1536]{0:T(1024)(128)(4,1)S(1)} %copy-done.15), kind=kOutput, calls=%fused_computation.12 | convolution fusion | flops 6453985280 | bytes 13633024 | tf_op jit(solution)/shard_map/dot_general | solution.py:12
  300.1 1.3 copy-done.19
  301.5 8.6 %fusion.32 = f32[1536,2048]{1,0:T(8,128)} fusion(bf16[1536,512]{0,1:T(8,128)(2,1)S(1)} %copy-done.19, bf16[2048,1408]{1,0:T(8,128)(2,1)} %bitcast.61), kind=kOutput, calls=%fused_computation.56 | convolution fusion | flops 3221225472 | bytes 16252928 | tf_op jit(solution)/shard_map/dot_general | solution.py:12
  310.1 8.2 %fusion.20 = f32[1536,2048]{1,0:T(8,128)} fusion(bf16[1536,512]{0,1:T(8,128)(2,1)S(1)} %copy-done.17, bf16[2048,1408]{1,0:T(8,128)(2,1)} %bitcast.55), kind=kOutput, calls=%fused_computation.44 | convolution fusion | flops 3221225472 | bytes 16252928 | tf_op jit(solution)/shard_map/dot_general | solution.py:12
  318.4 8.4 %fusion.18 = f32[1536,2048]{1,0:T(8,128)} fusion(bf16[1536,512]{0,1:T(8,128)(2,1)S(1)} %copy-done.23, bf16[2048,1408]{1,0:T(8,128)(2,1)} %bitcast.56), kind=kOutput, calls=%fused_computation.42 | convolution fusion | flops 3221225472 | bytes 16252928 | tf_op jit(solution)/shard_map/dot_general | solution.py:12
  326.7 13.9 %convolution_convert_fusion = bf16[1408,2048]{1,0:T(8,128)(2,1)} fusion(bf16[1536,512]{0,1:T(8,128)(2,1)S(1)} %copy-done.26, bf16[1536,512]{0,1:T(8,128)(2,1)S(1)} %copy-done.25, bf16[1536,384]{0,1:T(8,128)(2,1)S(1)} %copy-done.24, bf16[1536,2048]{1,0:T(8,128)(2,1)S(1)} %bitcast.50, f32[1536]{0:T(1024)S(1)} %mul.111), kind=kOutput, calls=%fused_computation.5 | convolution fusion | flops 8883666944 | bytes 16390144 | tf_op jit(solution)/shard_map/dot_general | solution.py:12
  340.6 1.2 copy-done.6
  341.9 7.8 %fusion.36 = f32[1536,2048]{1,0:T(8,128)} fusion(bf16[1536,384]{0,1:T(8,128)(2,1)S(1)} %copy-done.6, bf16[2048,1408]{1,0:T(8,128)(2,1)} %bitcast.57), kind=kOutput, calls=%fused_computation.60 | convolution fusion | flops 2415919104 | bytes 15335424 | tf_op jit(solution)/shard_map/dot_general | solution.py:12
  349.7 8.8 %fusion.28 = f32[1536,2048]{1,0:T(8,128)} fusion(bf16[1536,512]{0,1:T(8,128)(2,1)S(1)} %copy-done.21, bf16[2048,1408]{1,0:T(8,128)(2,1)} %bitcast.62), kind=kOutput, calls=%fused_computation.52 | convolution fusion | flops 3221225472 | bytes 16252928 | tf_op jit(solution)/shard_map/dot_general | solution.py:12
  358.5 24.7 %add_convert_fusion = bf16[1536,2048]{1,0:T(8,128)(2,1)} fusion(f32[1536,2048]{1,0:T(8,128)} %fusion.18, f32[1536,2048]{1,0:T(8,128)} %fusion.28, f32[1536,2048]{1,0:T(8,128)} %fusion.20, f32[1536,2048]{1,0:T(8,128)} %fusion.32, f32[1536,2048]{1,0:T(8,128)} %fusion.36, bf16[1536,384]{0,1:T(8,128)(2,1)S(1)} %copy-done.8, bf16[2048,1408]{1,0:T(8,128)(2,1)} %bitcast.63), kind=kOutput, calls=%fused_computation.3 | convolution fusion | flops 2434793472 | bytes 71958528 | tf_op jit(solution)/shard_map/dot_general | solution.py:12
  383.2 77.9 %all_to_all.21 = bf16[32,48,2048]{2,1,0:T(8,128)(2,1)S(1)} all-to-all(bf16[32,48,2048]{2,1,0:T(8,128)(2,1)} %bitcast.46), channel_id=1, replica_groups=mesh['dp'=4,'expert'=32] {'expert'}, dimensions={0} | all-to-all | bytes 12582912 | tf_op jit(solution)/shard_map/all_to_all | solution.py:90
  461.1 1.9 fusion.13
  462.9 1.3 multiply_convert_fusion.15
  464.2 1.4 multiply_convert_fusion.12
  465.6 1.4 multiply_convert_fusion.11
  467.0 1.8 maximum_bitcast_fusion
  468.9 2.8 fusion.41
  (89 shorter events, 1.0 us)
Async XLA Ops:
  7.2 83.3 %all-gather.5.cloned.1.call-start = ((), (), s32[]{:S(2)}) async-start(), calls=%async_computation.8 | async-start | bytes 17301504 | tf_op jit(solution)/shard_map/all_gather | solution.py:37
  7.9 159.6 %all-gather.7.cloned.1.call-start = ((), (), s32[]{:S(2)}) async-start(), calls=%async_computation.9 | async-start | bytes 17301504 | tf_op jit(solution)/shard_map/all_gather | solution.py:36
  9.4 0.9 copy-start.11
  10.2 0.6 copy-start.9
  25.8 11.0 %copy-start.13 = (s32[128,6]{0,1:T(8,128)S(1)}, s32[128,6]{0,1:T(8,128)}, u32[]{:S(2)}) copy-start(s32[128,6]{0,1:T(8,128)} %param.12) | copy-start | bytes 9220
  25.8 11.1 %copy-start.14 = (f32[128,6]{0,1:T(8,128)S(1)}, f32[128,6]{0,1:T(8,128)}, u32[]{:S(2)}) copy-start(f32[128,6]{0,1:T(8,128)} %param.11) | copy-start | bytes 9220
  28.2 53.2 %all-to-all-start = ((bf16[32,48,384]{2,1,0:T(8,128)(2,1)}), bf16[32,48,384]{2,1,0:T(8,128)(2,1)S(1)}, u32[]{:S(2)}, u32[]{:S(2)}) async-start(bf16[32,48,384]{2,1,0:T(8,128)(2,1)} %slice.104), calls=%async_computation | async-start | bytes 2359296 | tf_op jit(solution)/shard_map/all_to_all | solution.py:49
  81.4 124.2 %all-to-all-start.1 = ((bf16[32,48,512]{2,1,0:T(8,128)(2,1)}), bf16[32,48,512]{2,1,0:T(8,128)(2,1)}, u32[]{:S(2)}, u32[]{:S(2)}) async-start(bf16[32,48,512]{2,1,0:T(8,128)(2,1)} %get-tuple-element.15), calls=%async_computation.1 | async-start | bytes 3145728 | tf_op jit(solution)/shard_map/all_to_all | solution.py:49
  86.6 376.3 %reduce-scatter.5.cloned.1.call-start = ((), (), s32[]{:S(2)}) async-start(), calls=%async_computation.10 | async-start | bytes 3932160 | tf_op jit(solution)/shard_map/reduce_scatter | solution.py:83
  118.6 69.6 %copy-start.4 = (f32[1536,384]{0,1:T(8,128)S(1)}, f32[1536,384]{0,1:T(8,128)}, u32[]{:S(2)}) copy-start(f32[1536,384]{0,1:T(8,128)} %copy.37) | copy-start | bytes 7077892
  118.6 69.6 %copy-start.15 = (pred[1536]{0:T(1024)(128)(4,1)S(1)}, pred[1536]{0:T(1024)(128)(4,1)}, u32[]{:S(2)}) copy-start(pred[1536]{0:T(1024)(128)(4,1)} %broadcast_in_dim.88) | copy-start | bytes 4612
  188.2 10.1 %copy-start.1 = (bf16[1536,2048]{1,0:T(8,128)(2,1)S(1)}, bf16[1536,2048]{1,0:T(8,128)(2,1)}, u32[]{:S(2)}) copy-start(bf16[1536,2048]{1,0:T(8,128)(2,1)} %gather_fusion.1) | copy-start | bytes 18874372
  196.8 1.0 copy-start.5
  196.8 1.4 copy-start.7
  205.6 258.6 %reduce-scatter.7.cloned.1.call-start = ((), (), s32[]{:S(2)}) async-start(), calls=%async_computation.11 | async-start | bytes 5242880 | tf_op jit(solution)/shard_map/reduce_scatter | solution.py:83
  210.1 6.6 %copy-start.2 = (f32[1536,512]{0,1:T(8,128)S(1)}, f32[1536,512]{0,1:T(8,128)}, u32[]{:S(2)}) copy-start(f32[1536,512]{0,1:T(8,128)} %copy.40) | copy-start | bytes 9437188
  210.1 17.6 %slice-start.2 = ((s8[6291456]{0:T(1024)(128)(4,1)}), s8[4194304]{0:T(1024)(128)(4,1)S(1)}, s32[]{:S(2)}) async-start(s8[6291456]{0:T(1024)(128)(4,1)} %bitcast.51), calls=%async_computation.16 | async-start | bytes 8388608
  216.8 10.9 %slice-start.3 = ((s8[6291456]{0:T(1024)(128)(4,1)}), s8[2097152]{0:T(1024)(128)(4,1)S(1)}, s32[]{:S(2)}) async-start(s8[6291456]{0:T(1024)(128)(4,1)} %bitcast.51), calls=%async_computation.17 | async-start | bytes 4194304
  226.0 1.2 copy-start.16
  226.0 1.7 copy-start.18
  238.7 1.4 copy-start
  238.8 226.9 %reduce-scatter.9.cloned.1.call-start = ((), (), s32[]{:S(2)}) async-start(), calls=%async_computation.12 | async-start | bytes 5242880 | tf_op jit(solution)/shard_map/reduce_scatter | solution.py:83
  271.4 6.7 %copy-start.3 = (f32[1536,512]{0,1:T(8,128)S(1)}, f32[1536,512]{0,1:T(8,128)}, u32[]{:S(2)}) copy-start(f32[1536,512]{0,1:T(8,128)} %copy.43) | copy-start | bytes 9437188
  271.4 17.6 %slice-start.4 = ((s8[6291456]{0:T(1024)(128)(4,1)}), s8[4194304]{0:T(1024)(128)(4,1)S(1)}, s32[]{:S(2)}) async-start(s8[6291456]{0:T(1024)(128)(4,1)} %bitcast.53), calls=%async_computation.18 | async-start | bytes 8388608
  278.1 10.9 %slice-start.5 = ((s8[6291456]{0:T(1024)(128)(4,1)}), s8[2097152]{0:T(1024)(128)(4,1)S(1)}, s32[]{:S(2)}) async-start(s8[6291456]{0:T(1024)(128)(4,1)} %bitcast.53), calls=%async_computation.19 | async-start | bytes 4194304
  287.4 1.2 copy-start.20
  287.4 1.6 copy-start.22
  300.1 1.4 copy-start.19
  300.1 10.0 %copy-start.17 = (bf16[1536,512]{0,1:T(8,128)(2,1)S(1)}, bf16[1536,512]{0,1:T(8,128)(2,1)}, u32[]{:S(2)}) copy-start(bf16[1536,512]{0,1:T(8,128)(2,1)} %copy-done.16) | copy-start | bytes 4718596
  300.1 168.8 %reduce-scatter.11.cloned.1.call-start = ((), (), s32[]{:S(2)}) async-start(), calls=%async_computation.13 | async-start | bytes 7208960 | tf_op jit(solution)/shard_map/reduce_scatter | solution.py:88
  310.1 8.2 %copy-start.23 = (bf16[1536,512]{0,1:T(8,128)(2,1)S(1)}, bf16[1536,512]{0,1:T(8,128)(2,1)}, u32[]{:S(2)}) copy-start(bf16[1536,512]{0,1:T(8,128)(2,1)} %copy-done.22) | copy-start | bytes 4718596
  310.1 16.6 %slice-start = ((s8[6291456]{0:T(1024)(128)(4,1)}), s8[4194304]{0:T(1024)(128)(4,1)S(1)}, s32[]{:S(2)}) async-start(s8[6291456]{0:T(1024)(128)(4,1)} %bitcast.49), calls=%async_computation.14 | async-start | bytes 8388608
  318.3 8.4 %slice-start.1 = ((s8[6291456]{0:T(1024)(128)(4,1)}), s8[2097152]{0:T(1024)(128)(4,1)S(1)}, s32[]{:S(2)}) async-start(s8[6291456]{0:T(1024)(128)(4,1)} %bitcast.49), calls=%async_computation.15 | async-start | bytes 4194304
  318.3 8.4 %copy-start.24 = (bf16[1536,384]{0,1:T(8,128)(2,1)S(1)}, bf16[1536,384]{0,1:T(8,128)(2,1)}, u32[]{:S(2)}) copy-start(bf16[1536,384]{0,1:T(8,128)(2,1)} %get-tuple-element.12) | copy-start | bytes 3538948
  318.3 8.4 %copy-start.25 = (bf16[1536,512]{0,1:T(8,128)(2,1)S(1)}, bf16[1536,512]{0,1:T(8,128)(2,1)}, u32[]{:S(2)}) copy-start(bf16[1536,512]{0,1:T(8,128)(2,1)} %get-tuple-element.6) | copy-start | bytes 4718596
  318.3 8.4 %copy-start.26 = (bf16[1536,512]{0,1:T(8,128)(2,1)S(1)}, bf16[1536,512]{0,1:T(8,128)(2,1)}, u32[]{:S(2)}) copy-start(bf16[1536,512]{0,1:T(8,128)(2,1)} %get-tuple-element.9) | copy-start | bytes 4718596
  340.6 1.3 copy-start.6
  341.9 7.8 %copy-start.21 = (bf16[1536,512]{0,1:T(8,128)(2,1)S(1)}, bf16[1536,512]{0,1:T(8,128)(2,1)}, u32[]{:S(2)}) copy-start(bf16[1536,512]{0,1:T(8,128)(2,1)} %copy-done.20) | copy-start | bytes 4718596
  349.7 8.8 %copy-start.8 = (bf16[1536,384]{0,1:T(8,128)(2,1)S(1)}, bf16[1536,384]{0,1:T(8,128)(2,1)}, u32[]{:S(2)}) copy-start(bf16[1536,384]{0,1:T(8,128)(2,1)} %copy-done.7) | copy-start | bytes 3538948
  383.2 77.9 %copy-start.10 = (s32[32,128]{1,0:T(8,128)S(1)}, s32[32,128]{1,0:T(8,128)}, u32[]{:S(2)}) copy-start(s32[32,128]{1,0:T(8,128)} %copy-done.9) | copy-start | bytes 49156
  383.2 77.9 %copy-start.12 = (pred[32,128]{1,0:T(8,128)(4,1)S(1)}, pred[32,128]{1,0:T(8,128)(4,1)}, u32[]{:S(2)}) copy-start(pred[32,128]{1,0:T(8,128)(4,1)} %copy-done.11) | copy-start | bytes 12292
Sparse Core Ops, SparseCore 0:
  10.3 80.1 all-gather.4
  92.7 74.8 all-gather.6
  205.7 37.6 reduce-scatter.4
  245.7 46.5 reduce-scatter.6
  300.2 44.5 reduce-scatter.8
  347.1 59.4 reduce-scatter.10
where the time goes:
time: 485 us; the launch traced here: 479 us
  matrix products  160 us (33%)
  blocking collectives  144 us (30%)
  local copies, waits for them, and re-layouts  79.4 us (16%)
  waiting for transfers between devices  51.7 us (11%)
  other arithmetic  15.2 us (3%)
  between operations  14.6 us (3%)
  starting transfers between devices  14.3 us (3%)
    dot_general x19, matrix products, mm(): lax.dot_general(a, b, (((ca,), (cb,)), ((), ())), preferred_element_type=...  160 us
    all_to_all x1, blocking collectives, local(): lax.all_to_all(back, 'expert', split_axis=0, concat_axis=0, tiled=True)  77.9 us
    all_gather x1, waiting for transfers between devices, local(): rows_all = lax.all_gather(tokens, 'expert', axis=0, tiled=True)  49 us
    all_gather x1, blocking collectives, local(): meta_all = lax.all_gather(meta, 'expert', axis=0, tiled=False)  37.6 us
    all_to_all x1, blocking collectives, local(): lax.all_to_all(gate_rows[:, :, a:b], 'expert', split_axis=0, concat_axis=...  28.2 us
    gather x1, local copies, waits for them, and re-layouts, local(): grad_all[row_of_slot].astype(jnp.float32)  20.6 us
    gather x1, local copies, waits for them, and re-layouts, local(): rows_in = jnp.where(used[:, None], rows_all[row_of_slot], 0)  20.6 us
    unnamed x67, local copies, waits for them, and re-layouts  13.8 us
  transfers between devices with their start and end apart: 8, of which 2 were waited for; matrix products, arithmetic and copies ran while one was open for 51% of the time, Pallas kernels for 0%

commit v1 on v0

--- a/solution.py
+++ b/solution.py
@@ -33,8 +33,11 @@
     gate_mat, up_mat, down_mat = (w_gate[0], w_up[0], w_down[0])
     meta = jnp.concatenate([expert_ids.T.astype(jnp.float32), probs.T], axis=0)
     meta_all = lax.all_gather(meta, "expert", axis=0, tiled=False)
-    rows_all = lax.all_gather(tokens, "expert", axis=0, tiled=True)
-    grad_all = lax.all_gather(out_grad, "expert", axis=0, tiled=True)
+    rows_all, grad_all = jnp.split(
+        lax.all_gather(jnp.concatenate([tokens, out_grad], axis=1), "expert", axis=0, tiled=True),
+        [tokens.shape[1]],
+        axis=1,
+    )
     ids_t = expert_ids.T
     experts = lax.broadcasted_iota(jnp.int32, (n_peers, 1, 1), 0)
     named = ids_t[None] == experts

time: 485 us -> 524 us (1.080)
  local copies, waits for them, and re-layouts: 79.4 us -> 101 us
  waiting for transfers between devices: 51.7 us -> 67.5 us
    split x0 -> x1, local copies, waits for them, and re-layouts: none -> 23.5 us  [local(): jnp.split(lax.all_gather(jnp.concatenate([tokens, out_grad], axis=1), 'ex...]
    all_gather x2 -> x1, waiting for transfers between devices: 50.2 us -> 67.3 us  [local(): lax.all_gather(jnp.concatenate([tokens, out_grad], axis=1), 'expert', axi...]
    unnamed x67 -> x69, local copies, waits for them, and re-layouts: 13.8 us -> 12.6 us
  transfers between devices with their start and end apart: 8 -> 7, of which waited for: 2 -> 1; matrix products, arithmetic and copies ran while one was open for 51% -> 50% of each run, Pallas kernels for 0% -> 0%
where the time goes in v1:
time: 524 us; the launch traced here: 517 us
  matrix products  157 us (30%)
  blocking collectives  147 us (28%)
  local copies, waits for them, and re-layouts  101 us (19%)
  waiting for transfers between devices  67.5 us (13%)
  other arithmetic  16.2 us (3%)
  between operations  14.4 us (3%)
  starting transfers between devices  13.8 us (3%)
    dot_general x19, matrix products, mm(): lax.dot_general(a, b, (((ca,), (cb,)), ((), ())), preferred_element_type=...  157 us
    all_to_all x1, blocking collectives, local(): lax.all_to_all(back, 'expert', split_axis=0, concat_axis=0, tiled=True)  77.8 us
    all_gather x1, waiting for transfers between devices, local(): lax.all_gather(jnp.concatenate([tokens, out_grad], axis=1), 'expert', axi...  67.3 us
    all_gather x1, blocking collectives, local(): meta_all = lax.all_gather(meta, 'expert', axis=0, tiled=False)  41.2 us
    all_to_all x1, blocking collectives, local(): lax.all_to_all(gate_rows[:, :, a:b], 'expert', split_axis=0, concat_axis=...  28 us
    split x1, local copies, waits for them, and re-layouts, local(): jnp.split(lax.all_gather(jnp.concatenate([tokens, out_grad], axis=1), 'ex...  23.5 us
    gather x1, local copies, waits for them, and re-layouts, local(): rows_in = jnp.where(used[:, None], rows_all[row_of_slot], 0)  20.6 us
    gather x1, local copies, waits for them, and re-layouts, local(): grad_all[row_of_slot].astype(jnp.float32)  20.6 us
  transfers between devices with their start and end apart: 7, of which 1 were waited for; matrix products, arithmetic and copies ran while one was open for 50% of the time, Pallas kernels for 0%

profile of v1, /device:TPU:1, one launch (start us, length us, event | category | flops | bytes accessed | tf_op | source)
XLA Modules:
  0.0 517.0 jit_solution(4377698452091417062)
XLA Ops:
  7.2 2.4 pad_maximum_fusion
  9.8 0.1 convolution_convert_fusion.5
  9.9 0.4 copy-done.12
  10.3 0.6 copy-done.10
  10.9 0.6 select_reduce_fusion
  11.5 0.1 reshape.120
  11.6 2.8 copy.36
  14.4 3.6 reshape.119
  18.1 6.1 %gather_fusion.2 = bf16[1536,1408]{1,0:T(8,128)(2,1)} fusion(bf16[768,1408]{1,0:T(8,128)(2,1)S(1)} %reshape.119, s32[2048]{0:T(1024)S(1)} %pad_clamp_fusion), kind=kCustom, calls=%fused_computation.2 | custom fusion | bytes 8656896 | tf_op jit(solution)/shard_map/gather | solution.py:49
  24.2 2.6 slice.104
  26.8 8.5 %all-to-all-start = ((bf16[32,48,384]{2,1,0:T(8,128)(2,1)}), bf16[32,48,384]{2,1,0:T(8,128)(2,1)S(1)}, u32[]{:S(2)}, u32[]{:S(2)}) async-start(bf16[32,48,384]{2,1,0:T(8,128)(2,1)} %slice.104), calls=%async_computation | async-start | bytes 2359296 | tf_op jit(solution)/shard_map/all_to_all | solution.py:52
  35.3 41.2 %all-gather.1 = f32[32,12,128]{2,1,0:T(8,128)S(1)} all-gather(f32[1,12,128]{2,1,0:T(8,128)S(1)} %maximum_bitcast_fusion.2), channel_id=2, replica_groups=mesh['dp'=4,'expert'=32] {'expert'}, dimensions={0}, use_global_device_ids=true | all-gather | bytes 202752 | tf_op jit(solution)/shard_map/all_gather | solution.py:35
  76.7 0.1 convolution_convert_fusion.4
  76.8 0.3 select_reduce_fusion.2
  77.2 0.6 fusion.48
  77.9 0.7 broadcast_in_dim.88
  78.5 0.6 select_reduce_fusion.1
  79.2 0.1 add.88
  79.4 3.9 fusion.60
  83.3 4.7 all-to-all-start.1
  88.0 0.3 reduce-scatter.5.cloned.1.call-start
  88.4 0.3 bitcast_convert_fusion.2
  88.6 2.0 copy.37
  90.7 67.3 %all-gather.4.cloned.1.call-done = bf16[4096,4096]{1,0:T(8,128)(2,1)} async-done(((bf16[128,4096]{1,0:T(8,128)(2,1)}), bf16[4096,4096]{1,0:T(8,128)(2,1)}) %all-gather.4.cloned.1.call-update) | async-done | bytes 33554448 | tf_op jit(solution)/shard_map/all_gather | solution.py:37
  158.0 23.5 %fusion.59 = (bf16[4096,2048]{1,0:T(8,128)(2,1)}, bf16[4096,2048]{1,0:T(8,128)(2,1)}) fusion(bf16[4096,4096]{1,0:T(8,128)(2,1)} %all-gather.4.cloned.1.call-done), kind=kLoop, calls=%fused_computation.116 | loop fusion | bytes 67108864 | tf_op jit(solution)/shard_map/split | solution.py:36
  181.5 20.6 %gather_fusion.1 = bf16[1536,2048]{1,0:T(8,128)(2,1)} fusion(bf16[4096,2048]{1,0:T(8,128)(2,1)} %get-tuple-element.6, s32[2048]{0:T(1024)S(1)} %pad_clamp_fusion.1), kind=kCustom, calls=%fused_computation.1 | custom fusion | bytes 12589056 | tf_op jit(solution)/shard_map/gather | solution.py:67
  202.1 20.6 %gather_fusion = bf16[1536,2048]{1,0:T(8,128)(2,1)} fusion(bf16[4096,2048]{1,0:T(8,128)(2,1)} %get-tuple-element.7, s32[2048]{0:T(1024)S(1)} %pad_clamp_fusion.1), kind=kCustom, calls=%fused_computation | custom fusion | bytes 12589056 | tf_op jit(solution)/shard_map/gather | solution.py:68
  222.7 5.8 %fusion.38 = f32[1536,384]{0,1:T(8,128)S(1)} fusion(bf16[1,1408,2048]{2,1,0:T(8,128)(2,1)} %param.15, bf16[1536,2048]{1,0:T(8,128)(2,1)} %gather_fusion, f32[1536]{0:T(1024)S(1)} %mul.111), kind=kOutput, calls=%fused_computation.64 | convolution fusion | flops 2425356288 | bytes 10229760 | tf_op jit(solution)/shard_map/dot_general | solution.py:12
  228.5 7.2 %multiply_convert_fusion.8 = (bf16[1536,384]{0,1:T(8,128)(2,1)}, bf16[1536,384]{0,1:T(8,128)(2,1)S(1)}, bf16[1536,384]{0,1:T(8,128)(2,1)S(1)}) fusion(f32[1536,384]{0,1:T(8,128)S(1)} %copy-done.4, f32[1536,384]{0,1:T(8,128)S(1)} %fusion.38, bf16[2048,1408]{1,0:T(8,128)(2,1)} %bitcast.58, bf16[1536,2048]{1,0:T(8,128)(2,1)S(1)} %copy-done.1, ...), kind=kOutput, calls=%fused_computation.37 | convolution fusion | flops 2427912192 | bytes 16123392 | tf_op jit(solution)/shard_map/dot_general | solution.py:12
  235.7 1.0 copy-done.6
  236.7 0.4 copy-done.8
  237.1 7.3 %convolution_convert_fusion.3 = bf16[2048,768]{1,0:T(8,128)(2,1)} fusion(bf16[1536,384]{0,1:T(8,128)(2,1)S(1)} %get-tuple-element.16, bf16[1536,384]{0,1:T(8,128)(2,1)S(1)} %get-tuple-element.15, bf16[1536,2048]{1,0:T(8,128)(2,1)S(1)} %copy-done.1, pred[1536]{0:T(1024)(128)(4,1)S(1)} %copy-done.16), kind=kOutput, calls=%fused_computation.14 | convolution fusion | flops 4841275392 | bytes 11798016 | tf_op jit(solution)/shard_map/dot_general | solution.py:12
  244.5 1.8 bitcast_convert_fusion.1
  246.4 2.5 copy.40
  248.9 6.6 %fusion.24 = f32[1536,512]{0,1:T(8,128)S(1)} fusion(bf16[1,1408,2048]{2,1,0:T(8,128)(2,1)} %param.15, bf16[1536,2048]{1,0:T(8,128)(2,1)} %gather_fusion, f32[1536]{0:T(1024)S(1)} %mul.111), kind=kOutput, calls=%fused_computation.48 | convolution fusion | flops 3230662656 | bytes 11540480 | tf_op jit(solution)/shard_map/dot_general | solution.py:12
  255.6 9.3 %multiply_convert_fusion.2 = (bf16[1536,512]{0,1:T(8,128)(2,1)}, bf16[1536,512]{0,1:T(8,128)(2,1)S(1)}, bf16[1536,512]{0,1:T(8,128)(2,1)S(1)}) fusion(f32[1536,512]{0,1:T(8,128)S(1)} %copy-done.2, f32[1536,512]{0,1:T(8,128)S(1)} %fusion.24, bf16[2048,1408]{1,0:T(8,128)(2,1)} %bitcast.59, bf16[1536,2048]{1,0:T(8,128)(2,1)} %gather_fusion.1, ...), kind=kOutput, calls=%fused_computation.22 | convolution fusion | flops 3236167680 | bytes 19400192 | tf_op jit(solution)/shard_map/dot_general | solution.py:12
  264.8 1.1 copy-done.17
  266.0 0.6 copy-done.19
  266.5 11.0 %convolution_convert_fusion.2 = bf16[2048,1024]{1,0:T(8,128)(2,1)} fusion(bf16[1536,512]{0,1:T(8,128)(2,1)S(1)} %get-tuple-element.10, bf16[1536,512]{0,1:T(8,128)(2,1)S(1)} %get-tuple-element.9, bf16[1536,2048]{1,0:T(8,128)(2,1)S(1)} %bitcast.52, pred[1536]{0:T(1024)(128)(4,1)S(1)} %copy-done.16), kind=kOutput, calls=%fused_computation.13 | convolution fusion | flops 6453985280 | bytes 13633024 | tf_op jit(solution)/shard_map/dot_general | solution.py:12
  277.6 1.3 copy-done
  279.0 28.0 %all_to_all.20 = bf16[32,48,512]{2,1,0:T(8,128)(2,1)S(1)} all-to-all(bf16[32,48,512]{2,1,0:T(8,128)(2,1)S(1)} %copy-done), channel_id=1, replica_groups=mesh['dp'=4,'expert'=32] {'expert'}, dimensions={0} | all-to-all | bytes 3145728 | tf_op jit(solution)/shard_map/all_to_all | solution.py:52
  307.0 0.5 bitcast_convert_fusion
  307.5 2.5 copy.43
  310.0 6.7 %fusion.22 = f32[1536,512]{0,1:T(8,128)S(1)} fusion(bf16[1,1408,2048]{2,1,0:T(8,128)(2,1)} %param.15, bf16[1536,2048]{1,0:T(8,128)(2,1)} %gather_fusion, f32[1536]{0:T(1024)S(1)} %mul.111), kind=kOutput, calls=%fused_computation.46 | convolution fusion | flops 3230662656 | bytes 11540480 | tf_op jit(solution)/shard_map/dot_general | solution.py:12
  316.7 9.3 %multiply_convert_fusion.1 = (bf16[1536,512]{0,1:T(8,128)(2,1)}, bf16[1536,512]{0,1:T(8,128)(2,1)S(1)}, bf16[1536,512]{0,1:T(8,128)(2,1)S(1)}) fusion(f32[1536,512]{0,1:T(8,128)S(1)} %copy-done.3, f32[1536,512]{0,1:T(8,128)S(1)} %fusion.22, bf16[2048,1408]{1,0:T(8,128)(2,1)} %bitcast.60, bf16[1536,2048]{1,0:T(8,128)(2,1)} %gather_fusion.1, ...), kind=kOutput, calls=%fused_computation.21 | convolution fusion | flops 3236167680 | bytes 19400192 | tf_op jit(solution)/shard_map/dot_general | solution.py:12
  326.0 1.1 copy-done.21
  327.2 0.5 copy-done.23
  327.7 11.0 %convolution_convert_fusion.1 = bf16[2048,1024]{1,0:T(8,128)(2,1)} fusion(bf16[1536,512]{0,1:T(8,128)(2,1)S(1)} %get-tuple-element.13, bf16[1536,512]{0,1:T(8,128)(2,1)S(1)} %get-tuple-element.12, bf16[1536,2048]{1,0:T(8,128)(2,1)S(1)} %bitcast.54, pred[1536]{0:T(1024)(128)(4,1)S(1)} %copy-done.16), kind=kOutput, calls=%fused_computation.12 | convolution fusion | flops 6453985280 | bytes 13633024 | tf_op jit(solution)/shard_map/dot_general | solution.py:12
  338.8 1.3 copy-done.20
  340.2 8.6 %fusion.32 = f32[1536,2048]{1,0:T(8,128)} fusion(bf16[1536,512]{0,1:T(8,128)(2,1)S(1)} %copy-done.20, bf16[2048,1408]{1,0:T(8,128)(2,1)} %bitcast.61), kind=kOutput, calls=%fused_computation.56 | convolution fusion | flops 3221225472 | bytes 16252928 | tf_op jit(solution)/shard_map/dot_general | solution.py:12
  348.8 8.2 %fusion.20 = f32[1536,2048]{1,0:T(8,128)} fusion(bf16[1536,512]{0,1:T(8,128)(2,1)S(1)} %copy-done.18, bf16[2048,1408]{1,0:T(8,128)(2,1)} %bitcast.55), kind=kOutput, calls=%fused_computation.44 | convolution fusion | flops 3221225472 | bytes 16252928 | tf_op jit(solution)/shard_map/dot_general | solution.py:12
  357.0 8.4 %fusion.18 = f32[1536,2048]{1,0:T(8,128)} fusion(bf16[1536,512]{0,1:T(8,128)(2,1)S(1)} %copy-done.24, bf16[2048,1408]{1,0:T(8,128)(2,1)} %bitcast.56), kind=kOutput, calls=%fused_computation.42 | convolution fusion | flops 3221225472 | bytes 16252928 | tf_op jit(solution)/shard_map/dot_general | solution.py:12
  365.4 13.9 %convolution_convert_fusion = bf16[1408,2048]{1,0:T(8,128)(2,1)} fusion(bf16[1536,512]{0,1:T(8,128)(2,1)S(1)} %copy-done.27, bf16[1536,512]{0,1:T(8,128)(2,1)S(1)} %copy-done.26, bf16[1536,384]{0,1:T(8,128)(2,1)S(1)} %copy-done.25, bf16[1536,2048]{1,0:T(8,128)(2,1)S(1)} %bitcast.50, f32[1536]{0:T(1024)S(1)} %mul.111), kind=kOutput, calls=%fused_computation.5 | convolution fusion | flops 8883666944 | bytes 16390144 | tf_op jit(solution)/shard_map/dot_general | solution.py:12
  379.3 1.2 copy-done.7
  380.6 7.8 %fusion.36 = f32[1536,2048]{1,0:T(8,128)} fusion(bf16[1536,384]{0,1:T(8,128)(2,1)S(1)} %copy-done.7, bf16[2048,1408]{1,0:T(8,128)(2,1)} %bitcast.57), kind=kOutput, calls=%fused_computation.60 | convolution fusion | flops 2415919104 | bytes 15335424 | tf_op jit(solution)/shard_map/dot_general | solution.py:12
  388.4 8.8 %fusion.28 = f32[1536,2048]{1,0:T(8,128)} fusion(bf16[1536,512]{0,1:T(8,128)(2,1)S(1)} %copy-done.22, bf16[2048,1408]{1,0:T(8,128)(2,1)} %bitcast.62), kind=kOutput, calls=%fused_computation.52 | convolution fusion | flops 3221225472 | bytes 16252928 | tf_op jit(solution)/shard_map/dot_general | solution.py:12
  397.2 24.7 %add_convert_fusion = bf16[1536,2048]{1,0:T(8,128)(2,1)} fusion(f32[1536,2048]{1,0:T(8,128)} %fusion.18, f32[1536,2048]{1,0:T(8,128)} %fusion.28, f32[1536,2048]{1,0:T(8,128)} %fusion.20, f32[1536,2048]{1,0:T(8,128)} %fusion.32, f32[1536,2048]{1,0:T(8,128)} %fusion.36, bf16[1536,384]{0,1:T(8,128)(2,1)S(1)} %copy-done.9, bf16[2048,1408]{1,0:T(8,128)(2,1)} %bitcast.63), kind=kOutput, calls=%fused_computation.3 | convolution fusion | flops 2434793472 | bytes 71958528 | tf_op jit(solution)/shard_map/dot_general | solution.py:12
  421.9 77.8 %all_to_all.21 = bf16[32,48,2048]{2,1,0:T(8,128)(2,1)S(1)} all-to-all(bf16[32,48,2048]{2,1,0:T(8,128)(2,1)} %bitcast.46), channel_id=1, replica_groups=mesh['dp'=4,'expert'=32] {'expert'}, dimensions={0} | all-to-all | bytes 12582912 | tf_op jit(solution)/shard_map/all_to_all | solution.py:93
  499.7 1.9 fusion.13
  501.6 1.3 multiply_convert_fusion.15
  502.9 1.4 multiply_convert_fusion.12
  504.3 1.4 multiply_convert_fusion.11
  505.7 1.8 maximum_bitcast_fusion
  507.5 2.8 fusion.41
  (90 shorter events, 0.8 us)
Async XLA Ops:
  7.2 2.5 copy-start.14
  7.2 4.4 copy-start.5
  7.2 150.8 %all-gather.4.cloned.1.call-start = ((), (), s32[]{:S(2)}) async-start(), calls=%async_computation.8 | async-start | bytes 34603008 | tf_op jit(solution)/shard_map/all_gather | solution.py:37
  9.7 0.6 copy-start.12
  10.3 0.6 copy-start.10
  24.2 11.1 %copy-start.15 = (f32[128,6]{0,1:T(8,128)S(1)}, f32[128,6]{0,1:T(8,128)}, u32[]{:S(2)}) copy-start(f32[128,6]{0,1:T(8,128)} %param.11) | copy-start | bytes 9220
  26.8 56.5 %all-to-all-start = ((bf16[32,48,384]{2,1,0:T(8,128)(2,1)}), bf16[32,48,384]{2,1,0:T(8,128)(2,1)S(1)}, u32[]{:S(2)}, u32[]{:S(2)}) async-start(bf16[32,48,384]{2,1,0:T(8,128)(2,1)} %slice.104), calls=%async_computation | async-start | bytes 2359296 | tf_op jit(solution)/shard_map/all_to_all | solution.py:52
  83.3 161.2 %all-to-all-start.1 = ((bf16[32,48,512]{2,1,0:T(8,128)(2,1)}), bf16[32,48,512]{2,1,0:T(8,128)(2,1)}, u32[]{:S(2)}, u32[]{:S(2)}) async-start(bf16[32,48,512]{2,1,0:T(8,128)(2,1)} %get-tuple-element.17), calls=%async_computation.1 | async-start | bytes 3145728 | tf_op jit(solution)/shard_map/all_to_all | solution.py:52
  88.0 413.6 %reduce-scatter.5.cloned.1.call-start = ((), (), s32[]{:S(2)}) async-start(), calls=%async_computation.9 | async-start | bytes 3932160 | tf_op jit(solution)/shard_map/reduce_scatter | solution.py:86
  222.7 5.8 %copy-start.1 = (bf16[1536,2048]{1,0:T(8,128)(2,1)S(1)}, bf16[1536,2048]{1,0:T(8,128)(2,1)}, u32[]{:S(2)}) copy-start(bf16[1536,2048]{1,0:T(8,128)(2,1)} %gather_fusion.1) | copy-start | bytes 18874372
  222.7 5.8 %copy-start.4 = (f32[1536,384]{0,1:T(8,128)S(1)}, f32[1536,384]{0,1:T(8,128)}, u32[]{:S(2)}) copy-start(f32[1536,384]{0,1:T(8,128)} %copy.37) | copy-start | bytes 7077892
  222.7 5.8 %copy-start.16 = (pred[1536]{0:T(1024)(128)(4,1)S(1)}, pred[1536]{0:T(1024)(128)(4,1)}, u32[]{:S(2)}) copy-start(pred[1536]{0:T(1024)(128)(4,1)} %broadcast_in_dim.88) | copy-start | bytes 4612
  235.7 1.0 copy-start.6
  235.7 1.4 copy-start.8
  244.4 258.4 %reduce-scatter.7.cloned.1.call-start = ((), (), s32[]{:S(2)}) async-start(), calls=%async_computation.10 | async-start | bytes 5242880 | tf_op jit(solution)/shard_map/reduce_scatter | solution.py:86
  248.9 6.6 %copy-start.2 = (f32[1536,512]{0,1:T(8,128)S(1)}, f32[1536,512]{0,1:T(8,128)}, u32[]{:S(2)}) copy-start(f32[1536,512]{0,1:T(8,128)} %copy.40) | copy-start | bytes 9437188
  248.9 17.6 %slice-start.2 = ((s8[6291456]{0:T(1024)(128)(4,1)}), s8[4194304]{0:T(1024)(128)(4,1)S(1)}, s32[]{:S(2)}) async-start(s8[6291456]{0:T(1024)(128)(4,1)} %bitcast.51), calls=%async_computation.15 | async-start | bytes 8388608
  255.5 11.0 %slice-start.3 = ((s8[6291456]{0:T(1024)(128)(4,1)}), s8[2097152]{0:T(1024)(128)(4,1)S(1)}, s32[]{:S(2)}) async-start(s8[6291456]{0:T(1024)(128)(4,1)} %bitcast.51), calls=%async_computation.16 | async-start | bytes 4194304
  264.8 1.1 copy-start.17
  264.8 1.7 copy-start.19
  277.5 1.4 copy-start
  277.6 226.7 %reduce-scatter.9.cloned.1.call-start = ((), (), s32[]{:S(2)}) async-start(), calls=%async_computation.11 | async-start | bytes 5242880 | tf_op jit(solution)/shard_map/reduce_scatter | solution.py:86
  310.0 6.7 %copy-start.3 = (f32[1536,512]{0,1:T(8,128)S(1)}, f32[1536,512]{0,1:T(8,128)}, u32[]{:S(2)}) copy-start(f32[1536,512]{0,1:T(8,128)} %copy.43) | copy-start | bytes 9437188
  310.0 17.8 %slice-start.4 = ((s8[6291456]{0:T(1024)(128)(4,1)}), s8[4194304]{0:T(1024)(128)(4,1)S(1)}, s32[]{:S(2)}) async-start(s8[6291456]{0:T(1024)(128)(4,1)} %bitcast.53), calls=%async_computation.17 | async-start | bytes 8388608
  316.7 11.0 %slice-start.5 = ((s8[6291456]{0:T(1024)(128)(4,1)}), s8[2097152]{0:T(1024)(128)(4,1)S(1)}, s32[]{:S(2)}) async-start(s8[6291456]{0:T(1024)(128)(4,1)} %bitcast.53), calls=%async_computation.18 | async-start | bytes 4194304
  326.0 1.1 copy-start.21
  326.0 1.7 copy-start.23
  338.8 1.4 copy-start.20
  338.8 10.0 %copy-start.18 = (bf16[1536,512]{0,1:T(8,128)(2,1)S(1)}, bf16[1536,512]{0,1:T(8,128)(2,1)}, u32[]{:S(2)}) copy-start(bf16[1536,512]{0,1:T(8,128)(2,1)} %copy-done.17) | copy-start | bytes 4718596
  338.8 168.8 %reduce-scatter.11.cloned.1.call-start = ((), (), s32[]{:S(2)}) async-start(), calls=%async_computation.12 | async-start | bytes 7208960 | tf_op jit(solution)/shard_map/reduce_scatter | solution.py:91
  348.8 8.2 %copy-start.24 = (bf16[1536,512]{0,1:T(8,128)(2,1)S(1)}, bf16[1536,512]{0,1:T(8,128)(2,1)}, u32[]{:S(2)}) copy-start(bf16[1536,512]{0,1:T(8,128)(2,1)} %copy-done.23) | copy-start | bytes 4718596
  348.8 16.6 %slice-start = ((s8[6291456]{0:T(1024)(128)(4,1)}), s8[4194304]{0:T(1024)(128)(4,1)S(1)}, s32[]{:S(2)}) async-start(s8[6291456]{0:T(1024)(128)(4,1)} %bitcast.49), calls=%async_computation.13 | async-start | bytes 8388608
  357.0 8.4 %slice-start.1 = ((s8[6291456]{0:T(1024)(128)(4,1)}), s8[2097152]{0:T(1024)(128)(4,1)S(1)}, s32[]{:S(2)}) async-start(s8[6291456]{0:T(1024)(128)(4,1)} %bitcast.49), calls=%async_computation.14 | async-start | bytes 4194304
  357.0 8.4 %copy-start.25 = (bf16[1536,384]{0,1:T(8,128)(2,1)S(1)}, bf16[1536,384]{0,1:T(8,128)(2,1)}, u32[]{:S(2)}) copy-start(bf16[1536,384]{0,1:T(8,128)(2,1)} %get-tuple-element.14) | copy-start | bytes 3538948
  357.0 8.4 %copy-start.26 = (bf16[1536,512]{0,1:T(8,128)(2,1)S(1)}, bf16[1536,512]{0,1:T(8,128)(2,1)}, u32[]{:S(2)}) copy-start(bf16[1536,512]{0,1:T(8,128)(2,1)} %get-tuple-element.8) | copy-start | bytes 4718596
  357.0 8.4 %copy-start.27 = (bf16[1536,512]{0,1:T(8,128)(2,1)S(1)}, bf16[1536,512]{0,1:T(8,128)(2,1)}, u32[]{:S(2)}) copy-start(bf16[1536,512]{0,1:T(8,128)(2,1)} %get-tuple-element.11) | copy-start | bytes 4718596
  379.3 1.3 copy-start.7
  380.6 7.9 %copy-start.22 = (bf16[1536,512]{0,1:T(8,128)(2,1)S(1)}, bf16[1536,512]{0,1:T(8,128)(2,1)}, u32[]{:S(2)}) copy-start(bf16[1536,512]{0,1:T(8,128)(2,1)} %copy-done.21) | copy-start | bytes 4718596
  388.4 8.8 %copy-start.9 = (bf16[1536,384]{0,1:T(8,128)(2,1)S(1)}, bf16[1536,384]{0,1:T(8,128)(2,1)}, u32[]{:S(2)}) copy-start(bf16[1536,384]{0,1:T(8,128)(2,1)} %copy-done.8) | copy-start | bytes 3538948
  421.9 77.8 %copy-start.11 = (s32[32,128]{1,0:T(8,128)S(1)}, s32[32,128]{1,0:T(8,128)}, u32[]{:S(2)}) copy-start(s32[32,128]{1,0:T(8,128)} %copy-done.10) | copy-start | bytes 49156
  421.9 77.8 %copy-start.13 = (pred[32,128]{1,0:T(8,128)(4,1)S(1)}, pred[32,128]{1,0:T(8,128)(4,1)}, u32[]{:S(2)}) copy-start(pred[32,128]{1,0:T(8,128)(4,1)} %copy-done.12) | copy-start | bytes 12292
Sparse Core Ops, SparseCore 0:
  10.9 147.1 all-gather.3
  244.6 37.3 reduce-scatter.4
  284.4 46.5 reduce-scatter.6
  338.9 44.5 reduce-scatter.8
  385.7 59.4 reduce-scatter.10
